TPU v7x, 512 devices: a whole 4x4x16 slice. The times are simulated.
512 devices in a mesh: dp: 8 (over y, core), expert: 64 (over x, z).
Axes of the slice: x: 4, y: 4, z: 16, core: 2. Of those that a mesh axis runs over, the one named last changes fastest.
Arguments:
- tokens: bfloat16 [65536, 4096], P(('dp', 'expert')), may hold values from -6 to 6
- expert_ids: int32 [65536, 2], P(('dp', 'expert')), may hold values from 0 to 63, as said below
- gate_values: float32 [65536, 2], P(('dp', 'expert')), may hold values from 0.2 to 1
- w_gate: bfloat16 [4096, 14336], P('dp', 'expert'), may hold values from -0.09375 to 0.09375
- w_up: bfloat16 [4096, 14336], P('dp', 'expert'), may hold values from -0.09375 to 0.09375
- w_down: bfloat16 [14336, 4096], P('expert', 'dp'), may hold values from -0.046875 to 0.046875
- target: bfloat16 [65536, 4096], P(('dp', 'expert')), may hold values from -6 to 6
Outputs:
- token_grad: bfloat16 [65536, 4096], P(('dp', 'expert'))
- gate_grad: bfloat16 [4096, 14336], P('dp', 'expert')
- up_grad: bfloat16 [4096, 14336], P('dp', 'expert')
Inputs may be any that keep to these rules, and one draw needn't show every extreme that they name: `expert_ids`: A token's two expert ids differ, and no token names two experts below 1. Among the 128 tokens of one device each expert below 1 is named by 1 to 3 tokens, and in every draw some device names each of them exactly 3 times.
All inputs are finite; a program needn't handle non-finite values.
Results may differ from a plain program's by a relative error of at most 0.008.
Values may be sent and summed in bfloat16 or wider, within the bound.
A program may use at most 64 MiB of HBM per device.

v0:
```python
import jax
import jax.numpy as jnp
from jax import lax
from jax.sharding import PartitionSpec as P

EXPERTS = 1


def contract_last(matrix_a, matrix_b):
    return lax.dot_general(
        matrix_a, matrix_b, (((1,), (1,)), ((), ())), preferred_element_type=jnp.float32
    )


def rounded_terms(column_blocks, grad_blocks):
    terms = jnp.einsum(
        "krd,krh->kdh", column_blocks, grad_blocks, preferred_element_type=jnp.float32
    )
    terms = lax.optimization_barrier(terms.astype(jnp.bfloat16))
    return jnp.sum(terms.astype(jnp.float32), axis=0)


def spread_rows(rows, group_size, capacity, features):
    flat = rows.reshape(EXPERTS, 1, capacity * features)
    wide = jnp.broadcast_to(flat, (EXPERTS, group_size, capacity * features))
    return wide.reshape(EXPERTS * group_size * capacity, features)


def fold_group(rows, group_size, capacity, features):
    shaped = rows.reshape(EXPERTS, group_size, capacity * features).astype(jnp.float32)
    return jnp.sum(shaped, axis=1).reshape(EXPERTS * capacity, features)


def shards(tokens, expert_ids, gate_values, w_gate, w_up, w_down, target):
    devices_along = lax.axis_size("expert")
    group_size = devices_along // EXPERTS
    tok_rows = tokens.shape[0]
    features = tokens.shape[1]
    hid_local = w_gate.shape[1]
    capacity = max(2, 3 * tok_rows // 128)
    slot_total = EXPERTS * capacity
    flat_ids = expert_ids.reshape(-1)
    pair_count = flat_ids.shape[0]
    window = flat_ids < EXPERTS
    onehot = (flat_ids[:, None] == jnp.arange(EXPERTS, dtype=jnp.int32)[None, :]).astype(jnp.int32)
    slot_index = jnp.sum((jnp.cumsum(onehot, axis=0) - onehot) * onehot, axis=1)
    position = jnp.where(window, flat_ids * capacity + slot_index, slot_total)
    owning = jnp.arange(pair_count, dtype=jnp.int32) // 2
    slot_token = jnp.zeros((slot_total + 1,), jnp.int32).at[position].set(owning)[:slot_total]
    slot_live = jnp.zeros((slot_total + 1,), jnp.bool_).at[position].set(True)[:slot_total]
    slot_gate = (
        jnp.zeros((slot_total + 1,), jnp.float32)
        .at[position]
        .set(gate_values.reshape(-1))[:slot_total]
    )
    safe_pairs = jnp.minimum(position, slot_total - 1).reshape(tok_rows, 2)
    live_pairs = window.reshape(tok_rows, 2)

    def pick(table, column):
        return jnp.where(live_pairs[:, column : column + 1], table[safe_pairs[:, column]], 0.0)

    outgoing = jnp.where(slot_live[:, None], tokens[slot_token], jnp.zeros((), tokens.dtype))
    outgoing = spread_rows(outgoing, group_size, capacity, features)
    received = lax.all_to_all(outgoing, "expert", split_axis=0, concat_axis=0, tiled=True)
    rows_count = received.shape[0]
    full_gate, full_up, full_down = (
        lax.all_gather(w_gate, "dp", axis=0, tiled=True),
        lax.all_gather(w_up, "dp", axis=0, tiled=True),
        lax.all_gather(w_down, "dp", axis=1, tiled=True),
    )
    gate_pre = jnp.dot(received, full_gate, preferred_element_type=jnp.float32)
    up_pre = jnp.dot(received, full_up, preferred_element_type=jnp.float32)
    sigmoid_gate = jax.nn.sigmoid(gate_pre)
    activated = sigmoid_gate * gate_pre
    hidden = (activated * up_pre).astype(jnp.bfloat16)
    partial_out = jnp.dot(hidden, full_down, preferred_element_type=jnp.float32).astype(
        jnp.bfloat16
    )
    returned_out = lax.all_to_all(partial_out, "expert", split_axis=0, concat_axis=0, tiled=True)
    expert_out = fold_group(returned_out, group_size, capacity, features)
    combined = gate_values[:, 0:1] * pick(expert_out, 0) + gate_values[:, 1:2] * pick(expert_out, 1)
    residual = combined - target.astype(jnp.float32)
    outgoing_grad = jnp.where(
        slot_live[:, None], slot_gate[:, None] * residual[slot_token], 0.0
    ).astype(jnp.bfloat16)
    outgoing_grad = spread_rows(outgoing_grad, group_size, capacity, features)
    cotangent = lax.all_to_all(outgoing_grad, "expert", split_axis=0, concat_axis=0, tiled=True)
    grad_hidden = contract_last(cotangent, full_down)
    derivative = sigmoid_gate * (1.0 + gate_pre * (1.0 - sigmoid_gate))
    grad_gate_pre = (grad_hidden * up_pre * derivative).astype(jnp.bfloat16)
    grad_up_pre = (grad_hidden * activated).astype(jnp.bfloat16)
    row_part = (
        contract_last(grad_gate_pre, full_gate) + contract_last(grad_up_pre, full_up)
    ).astype(jnp.bfloat16)
    back_rows = lax.all_to_all(row_part, "expert", split_axis=0, concat_axis=0, tiled=True)
    row_grad = fold_group(back_rows, group_size, capacity, features)
    token_grad = (pick(row_grad, 0) + pick(row_grad, 1)).astype(jnp.bfloat16)
    shard_columns = lax.all_to_all(received, "dp", split_axis=1, concat_axis=0, tiled=True)
    shard_width = shard_columns.shape[1]
    dp_count = lax.axis_size("dp")
    every_gate, every_up = (
        lax.all_gather(grad_gate_pre, "dp", axis=0, tiled=True),
        lax.all_gather(grad_up_pre, "dp", axis=0, tiled=True),
    )
    column_blocks = shard_columns.reshape(dp_count, rows_count, shard_width)
    gate_sum = rounded_terms(column_blocks, every_gate.reshape(dp_count, rows_count, hid_local))
    up_sum = rounded_terms(column_blocks, every_up.reshape(dp_count, rows_count, hid_local))
    return (token_grad, gate_sum.astype(jnp.bfloat16), up_sum.astype(jnp.bfloat16))


def solution(mesh):
    placed = (
        P(("dp", "expert"), None),
        P(("dp", "expert"), None),
        P(("dp", "expert"), None),
        P("dp", "expert"),
        P("dp", "expert"),
        P("expert", "dp"),
        P(("dp", "expert"), None),
    )
    return jax.shard_map(
        shards,
        mesh=mesh,
        in_specs=placed,
        out_specs=(P(("dp", "expert"), None), P("dp", "expert"), P("dp", "expert")),
        check_vma=False,
    )
```

profile of v0, /device:TPU:6, one launch (start us, length us, event | category | flops | bytes accessed | tf_op | source)
XLA Modules:
  0.0 524.1 jit_solution(15885397472876217078)
XLA Ops:
  7.2 0.7 all-gather.6.cloned.1.call-update
  7.9 0.8 copy.16
  10.4 1.4 scatter_custom_fusion.2
  11.8 1.5 scatter_custom_fusion
  13.4 0.6 gather_fusion
  14.0 2.4 broadcast_in_dim.87
  16.4 18.8 %all-to-all-start = ((bf16[64,3,4096]{2,1,0:T(4,128)(2,1)}), bf16[64,3,4096]{2,1,0:T(4,128)(2,1)S(1)}, u32[]{:S(2)}, u32[]{:S(2)}) async-start(bf16[64,3,4096]{2,1,0:T(4,128)(2,1)} %broadcast_in_dim.87), calls=%async_computation | async-start | bytes 4194304 | tf_op jit(solution)/shard_map/all_to_all | solution.py:64
  35.2 0.7 all-gather.4.cloned.1.call-update
  36.0 0.7 all-gather.8.cloned.1.call-update
  36.7 95.8 %all-to-all-done = bf16[64,3,4096]{2,1,0:T(4,128)(2,1)S(1)} async-done(((bf16[64,3,4096]{2,1,0:T(4,128)(2,1)}), bf16[64,3,4096]{2,1,0:T(4,128)(2,1)S(1)}, u32[]{:S(2)}, u32[]{:S(2)}) %all-to-all-start) | async-done | bytes 1572896 | tf_op jit(solution)/shard_map/all_to_all | solution.py:64
  132.5 2.5 all_to_all.37
  135.0 2.7 fusion.16
  137.8 3.4 fusion.15
  141.2 3.4 convolution_convert_fusion
  144.5 4.1 all_to_all.38
  148.6 8.6 %all-to-all-start.1 = ((bf16[64,3,4096]{2,1,0:T(4,128)(2,1)}), bf16[64,3,4096]{2,1,0:T(4,128)(2,1)}, u32[]{:S(2)}, u32[]{:S(2)}) async-start(bf16[64,3,4096]{2,1,0:T(4,128)(2,1)} %all_to_all.38), calls=%async_computation.1 | async-start | bytes 4194304 | tf_op jit(solution)/shard_map/all_to_all | solution.py:79
  157.5 1.6 scatter_custom_fusion.1
  159.5 94.7 %all-to-all-done.1 = bf16[64,3,4096]{2,1,0:T(4,128)(2,1)} async-done(((bf16[64,3,4096]{2,1,0:T(4,128)(2,1)}), bf16[64,3,4096]{2,1,0:T(4,128)(2,1)}, u32[]{:S(2)}, u32[]{:S(2)}) %all-to-all-start.1) | async-done | bytes 1572896 | tf_op jit(solution)/shard_map/all_to_all | solution.py:79
  254.2 2.5 convert_reduce_fusion.1
  256.7 2.3 gather_fusion.2
  259.0 2.4 gather_fusion.1
  261.3 4.6 convert_subtract_fusion
  265.9 2.2 gather_fusion.3
  268.2 2.3 broadcast_in_dim.92
  270.5 8.8 %all-to-all-start.2 = ((bf16[64,3,4096]{2,1,0:T(4,128)(2,1)}), bf16[64,3,4096]{2,1,0:T(4,128)(2,1)}, u32[]{:S(2)}, u32[]{:S(2)}) async-start(bf16[64,3,4096]{2,1,0:T(4,128)(2,1)} %broadcast_in_dim.92), calls=%async_computation.2 | async-start | bytes 4194304 | tf_op jit(solution)/shard_map/all_to_all | solution.py:87
  279.3 3.1 all_to_all.44
  282.4 3.0 copy.20
  285.4 90.8 %all-to-all-done.2 = bf16[64,3,4096]{2,1,0:T(4,128)(2,1)} async-done(((bf16[64,3,4096]{2,1,0:T(4,128)(2,1)}), bf16[64,3,4096]{2,1,0:T(4,128)(2,1)}, u32[]{:S(2)}, u32[]{:S(2)}) %all-to-all-start.2) | async-done | bytes 1572896 | tf_op jit(solution)/shard_map/all_to_all | solution.py:87
  376.2 4.5 all-to-all-start.4
  380.7 4.3 all_to_all.41
  385.0 2.8 multiply_convert_fusion
  387.9 0.6 fusion.17
  388.5 0.9 copy-done.1
  389.4 1.8 fusion
  391.2 4.1 all_to_all.42
  395.2 7.0 %all-to-all-done.4 = bf16[192,8,512]{2,0,1:T(8,128)(2,1)S(1)} async-done(((bf16[192,8,512]{2,0,1:T(8,128)(2,1)}), bf16[192,8,512]{2,0,1:T(8,128)(2,1)S(1)}, u32[]{:S(2)}, u32[]{:S(2)}) %all-to-all-start.4) | async-done | bytes 1572896 | tf_op jit(solution)/shard_map/all_to_all | solution.py:98
  402.2 8.9 %all-to-all-start.3 = ((bf16[64,3,4096]{2,1,0:T(4,128)(2,1)}), bf16[64,3,4096]{2,1,0:T(4,128)(2,1)}, u32[]{:S(2)}, u32[]{:S(2)}) async-start(bf16[64,3,4096]{2,1,0:T(4,128)(2,1)} %all_to_all.42), calls=%async_computation.3 | async-start | bytes 4194304 | tf_op jit(solution)/shard_map/all_to_all | solution.py:95
  411.1 13.4 %all_gather.19 = bf16[1536,224]{1,0:T(8,128)(2,1)S(1)} all-gather(bf16[192,224]{1,0:T(8,128)(2,1)S(1)} %get-tuple-element.11), channel_id=1, replica_groups=mesh['dp'=8,'expert'=64] {'dp'}, dimensions={0}, use_global_device_ids=true | all-gather | bytes 774144 | tf_op jit(solution)/shard_map/all_gather | solution.py:103
  424.5 2.1 convolution_convert_fusion.1
  426.6 13.6 %all_gather.18 = bf16[1536,224]{1,0:T(8,128)(2,1)S(1)} all-gather(bf16[192,224]{1,0:T(8,128)(2,1)S(1)} %get-tuple-element.12), channel_id=1, replica_groups=mesh['dp'=8,'expert'=64] {'dp'}, dimensions={0}, use_global_device_ids=true | all-gather | bytes 774144 | tf_op jit(solution)/shard_map/all_gather | solution.py:102
  440.2 2.1 convolution_convert_fusion.2
  442.3 2.6 reduce_sum.49
  444.9 1.0 reduce_sum.48
  445.9 62.7 %all-to-all-done.3 = bf16[64,3,4096]{2,1,0:T(4,128)(2,1)} async-done(((bf16[64,3,4096]{2,1,0:T(4,128)(2,1)}), bf16[64,3,4096]{2,1,0:T(4,128)(2,1)}, u32[]{:S(2)}, u32[]{:S(2)}) %all-to-all-start.3) | async-done | bytes 1572896 | tf_op jit(solution)/shard_map/all_to_all | solution.py:95
  508.6 2.5 convert_reduce_fusion
  511.1 1.2 gather_fusion.5
  512.2 2.4 gather_fusion.4
  514.6 3.0 add_convert_fusion
  (43 shorter events, 2.6 us)
Async XLA Ops:
  7.2 6.2 %copy-start = (bf16[128,4096]{1,0:T(8,128)(2,1)S(1)}, bf16[128,4096]{1,0:T(8,128)(2,1)}, u32[]{:S(2)}) copy-start(bf16[128,4096]{1,0:T(8,128)(2,1)} %param.7) | copy-start | bytes 3145732
  7.2 127.9 %all-gather.6.cloned.1.call-start = ((), (), s32[]{:S(2)}) async-start(), calls=%async_computation.6 | async-start | bytes 2064384 | tf_op jit(solution)/shard_map/all_gather | solution.py:68
  16.4 116.1 %all-to-all-start = ((bf16[64,3,4096]{2,1,0:T(4,128)(2,1)}), bf16[64,3,4096]{2,1,0:T(4,128)(2,1)S(1)}, u32[]{:S(2)}, u32[]{:S(2)}) async-start(bf16[64,3,4096]{2,1,0:T(4,128)(2,1)} %broadcast_in_dim.87), calls=%async_computation | async-start | bytes 4194304 | tf_op jit(solution)/shard_map/all_to_all | solution.py:64
  35.2 102.6 %all-gather.4.cloned.1.call-start = ((), (), s32[]{:S(2)}) async-start(), calls=%async_computation.5 | async-start | bytes 2064384 | tf_op jit(solution)/shard_map/all_gather | solution.py:67
  35.9 105.2 %all-gather.8.cloned.1.call-start = ((), (), s32[]{:S(2)}) async-start(), calls=%async_computation.7 | async-start | bytes 2064384 | tf_op jit(solution)/shard_map/all_gather | solution.py:69
  148.6 8.6 %copy-start.5 = (f32[128,2]{0,1:T(2,128)S(1)}, f32[128,2]{0,1:T(2,128)}, u32[]{:S(2)}) copy-start(f32[128,2]{0,1:T(2,128)} %param.9) | copy-start | bytes 3076
  148.6 105.6 %all-to-all-start.1 = ((bf16[64,3,4096]{2,1,0:T(4,128)(2,1)}), bf16[64,3,4096]{2,1,0:T(4,128)(2,1)}, u32[]{:S(2)}, u32[]{:S(2)}) async-start(bf16[64,3,4096]{2,1,0:T(4,128)(2,1)} %all_to_all.38), calls=%async_computation.1 | async-start | bytes 4194304 | tf_op jit(solution)/shard_map/all_to_all | solution.py:79
  270.5 105.7 %all-to-all-start.2 = ((bf16[64,3,4096]{2,1,0:T(4,128)(2,1)}), bf16[64,3,4096]{2,1,0:T(4,128)(2,1)}, u32[]{:S(2)}, u32[]{:S(2)}) async-start(bf16[64,3,4096]{2,1,0:T(4,128)(2,1)} %broadcast_in_dim.92), calls=%async_computation.2 | async-start | bytes 4194304 | tf_op jit(solution)/shard_map/all_to_all | solution.py:87
  376.2 26.0 %all-to-all-start.4 = ((bf16[192,8,512]{2,0,1:T(8,128)(2,1)}), bf16[192,8,512]{2,0,1:T(8,128)(2,1)S(1)}, u32[]{:S(2)}, u32[]{:S(2)}) async-start(bf16[192,8,512]{2,0,1:T(8,128)(2,1)} %copy.20), calls=%async_computation.4 | async-start | bytes 3145728 | tf_op jit(solution)/shard_map/all_to_all | solution.py:98
  380.7 4.3 copy-start.4
  385.0 2.8 copy-start.2
  387.9 1.5 copy-start.1
  402.2 106.4 %all-to-all-start.3 = ((bf16[64,3,4096]{2,1,0:T(4,128)(2,1)}), bf16[64,3,4096]{2,1,0:T(4,128)(2,1)}, u32[]{:S(2)}, u32[]{:S(2)}) async-start(bf16[64,3,4096]{2,1,0:T(4,128)(2,1)} %all_to_all.42), calls=%async_computation.3 | async-start | bytes 4194304 | tf_op jit(solution)/shard_map/all_to_all | solution.py:95
  442.3 2.6 copy-start.3
Sparse Core Ops, SparseCore 0:
  10.1 36.9 all-gather.5
  49.2 32.8 all-gather.3
  84.3 32.8 all-gather.7
where the time goes:
time: 525 us; the launch traced here: 524 us
  waiting for transfers between devices  353 us (67%)
  starting transfers between devices  49.6 us (9%)
  local copies, waits for them, and re-layouts  44.5 us (8%)
  blocking collectives  27 us (5%)
  matrix products  18.8 us (4%)
  other arithmetic  17 us (3%)
  between operations  14 us (3%)
    all_to_all x1, waiting for transfers between devices, shards(): lax.all_to_all(outgoing, 'expert', split_axis=0, concat_axis=0, tiled=True)  95.8 us
    all_to_all x1, waiting for transfers between devices, shards(): lax.all_to_all(partial_out, 'expert', split_axis=0, concat_axis=0, tiled=...  94.7 us
    all_to_all x1, waiting for transfers between devices, shards(): lax.all_to_all(outgoing_grad, 'expert', split_axis=0, concat_axis=0, tile...  90.8 us
    all_to_all x1, waiting for transfers between devices, shards(): lax.all_to_all(row_part, 'expert', split_axis=0, concat_axis=0, tiled=True)  62.7 us
    all_to_all x1, starting transfers between devices, shards(): lax.all_to_all(outgoing, 'expert', split_axis=0, concat_axis=0, tiled=True)  18.8 us
    all_gather x1, blocking collectives, shards(): lax.all_gather(grad_gate_pre, 'dp', axis=0, tiled=True)  13.6 us
    all_gather x1, blocking collectives, shards(): lax.all_gather(grad_up_pre, 'dp', axis=0, tiled=True)  13.4 us
  transfers between devices with their start and end apart: 8, of which 5 were waited for; matrix products, arithmetic and copies ran while one was open for 6% of the time, Pallas kernels for 0%

commit v1 on v0

--- a/solution.py
+++ b/solution.py
@@ -2,6 +2,7 @@
 import jax.numpy as jnp
 from jax import lax
 from jax.sharding import PartitionSpec as P
+from jax.lax import all_to_all, axis_size
 
 EXPERTS = 1
 
@@ -99,7 +100,15 @@
     shard_width = shard_columns.shape[1]
     dp_count = lax.axis_size("dp")
     every_gate, every_up = (
-        lax.all_gather(grad_gate_pre, "dp", axis=0, tiled=True),
+        jnp.concatenate(
+            all_to_all(
+                jnp.stack([grad_gate_pre for _ in range(axis_size("dp"))], axis=0),
+                concat_axis=0,
+                split_axis=0,
+                axis_name="dp",
+            ),
+            0,
+        ),
         lax.all_gather(grad_up_pre, "dp", axis=0, tiled=True),
     )
     column_blocks = shard_columns.reshape(dp_count, rows_count, shard_width)

time: 525 us -> 543 us (1.034)
  waiting for transfers between devices: 353 us -> 378 us
  blocking collectives: 27 us -> 13.6 us
    all_gather x1 -> x0, blocking collectives: 13.6 us -> none  [shards(): lax.all_gather(grad_gate_pre, 'dp', axis=0, tiled=True)]
    all_to_all x1, waiting for transfers between devices: 62.7 us -> 74.7 us  [shards(): lax.all_to_all(row_part, 'expert', split_axis=0, concat_axis=0, tiled=True)]
    all_to_all x1, waiting for transfers between devices: 7 us -> 14.5 us  [shards(): lax.all_to_all(received, 'dp', split_axis=1, concat_axis=0, tiled=True)]
  transfers between devices with their start and end apart: 8 -> 9, of which waited for: 5 -> 6; matrix products, arithmetic and copies ran while one was open for 6% -> 7% of each run, Pallas kernels for 0% -> 0%
where the time goes in v1:
time: 543 us; the launch traced here: 542 us
  waiting for transfers between devices  378 us (70%)
  starting transfers between devices  53.2 us (10%)
  local copies, waits for them, and re-layouts  44.6 us (8%)
  matrix products  20.4 us (4%)
  other arithmetic  18.4 us (3%)
  between operations  14 us (3%)
  blocking collectives  13.6 us (3%)
    all_to_all x1, waiting for transfers between devices, shards(): lax.all_to_all(outgoing, 'expert', split_axis=0, concat_axis=0, tiled=True)  95.8 us
    all_to_all x1, waiting for transfers between devices, shards(): lax.all_to_all(partial_out, 'expert', split_axis=0, concat_axis=0, tiled=...  94.7 us
    all_to_all x1, waiting for transfers between devices, shards(): lax.all_to_all(outgoing_grad, 'expert', split_axis=0, concat_axis=0, tile...  90.8 us
    all_to_all x1, waiting for transfers between devices, shards(): lax.all_to_all(row_part, 'expert', split_axis=0, concat_axis=0, tiled=True)  74.7 us
    all_to_all x1, starting transfers between devices, shards(): lax.all_to_all(outgoing, 'expert', split_axis=0, concat_axis=0, tiled=True)  18.8 us
    all_to_all x1, waiting for transfers between devices, shards(): lax.all_to_all(received, 'dp', split_axis=1, concat_axis=0, tiled=True)  14.5 us
    all_gather x1, blocking collectives, shards(): lax.all_gather(grad_up_pre, 'dp', axis=0, tiled=True)  13.6 us
  transfers between devices with their start and end apart: 9, of which 6 were waited for; matrix products, arithmetic and copies ran while one was open for 7% of the time, Pallas kernels for 0%

profile of v1, /device:TPU:6, one launch (start us, length us, event | category | flops | bytes accessed | tf_op | source)
XLA Modules:
  0.0 541.7 jit_solution(895550880512408620)
XLA Ops:
  7.2 0.7 all-gather.6.cloned.1.call-update
  7.9 0.8 copy.16
  10.4 1.4 scatter_custom_fusion.2
  11.8 1.5 scatter_custom_fusion
  14.0 2.4 broadcast_in_dim.87
  16.4 18.8 %all-to-all-start = ((bf16[64,3,4096]{2,1,0:T(4,128)(2,1)}), bf16[64,3,4096]{2,1,0:T(4,128)(2,1)S(1)}, u32[]{:S(2)}, u32[]{:S(2)}) async-start(bf16[64,3,4096]{2,1,0:T(4,128)(2,1)} %broadcast_in_dim.87), calls=%async_computation | async-start | bytes 4194304 | tf_op jit(solution)/shard_map/all_to_all | solution.py:65
  35.2 0.7 all-gather.4.cloned.1.call-update
  36.0 0.7 all-gather.8.cloned.1.call-update
  36.7 95.8 %all-to-all-done = bf16[64,3,4096]{2,1,0:T(4,128)(2,1)S(1)} async-done(((bf16[64,3,4096]{2,1,0:T(4,128)(2,1)}), bf16[64,3,4096]{2,1,0:T(4,128)(2,1)S(1)}, u32[]{:S(2)}, u32[]{:S(2)}) %all-to-all-start) | async-done | bytes 1572896 | tf_op jit(solution)/shard_map/all_to_all | solution.py:65
  132.5 2.5 all_to_all.40
  135.0 2.7 fusion.16
  137.8 3.4 fusion.15
  141.2 3.4 convolution_convert_fusion
  144.5 4.1 all_to_all.41
  148.6 8.6 %all-to-all-start.1 = ((bf16[64,3,4096]{2,1,0:T(4,128)(2,1)}), bf16[64,3,4096]{2,1,0:T(4,128)(2,1)}, u32[]{:S(2)}, u32[]{:S(2)}) async-start(bf16[64,3,4096]{2,1,0:T(4,128)(2,1)} %all_to_all.41), calls=%async_computation.1 | async-start | bytes 4194304 | tf_op jit(solution)/shard_map/all_to_all | solution.py:80
  157.5 1.6 scatter_custom_fusion.1
  159.5 94.7 %all-to-all-done.1 = bf16[64,3,4096]{2,1,0:T(4,128)(2,1)} async-done(((bf16[64,3,4096]{2,1,0:T(4,128)(2,1)}), bf16[64,3,4096]{2,1,0:T(4,128)(2,1)}, u32[]{:S(2)}, u32[]{:S(2)}) %all-to-all-start.1) | async-done | bytes 1572896 | tf_op jit(solution)/shard_map/all_to_all | solution.py:80
  254.2 2.5 convert_reduce_fusion.1
  256.6 2.3 gather_fusion.2
  258.9 2.4 gather_fusion.1
  261.3 4.6 convert_subtract_fusion
  265.9 2.2 gather_fusion.3
  268.2 2.3 broadcast_in_dim.92
  270.5 8.8 %all-to-all-start.2 = ((bf16[64,3,4096]{2,1,0:T(4,128)(2,1)}), bf16[64,3,4096]{2,1,0:T(4,128)(2,1)}, u32[]{:S(2)}, u32[]{:S(2)}) async-start(bf16[64,3,4096]{2,1,0:T(4,128)(2,1)} %broadcast_in_dim.92), calls=%async_computation.2 | async-start | bytes 4194304 | tf_op jit(solution)/shard_map/all_to_all | solution.py:88
  279.3 3.1 all_to_all.47
  282.4 3.0 copy.20
  285.4 90.8 %all-to-all-done.2 = bf16[64,3,4096]{2,1,0:T(4,128)(2,1)} async-done(((bf16[64,3,4096]{2,1,0:T(4,128)(2,1)}), bf16[64,3,4096]{2,1,0:T(4,128)(2,1)}, u32[]{:S(2)}, u32[]{:S(2)}) %all-to-all-start.2) | async-done | bytes 1572896 | tf_op jit(solution)/shard_map/all_to_all | solution.py:88
  376.2 4.5 all-to-all-start.4
  380.7 4.3 all_to_all.44
  385.0 2.7 multiply_convert_fusion
  387.8 14.5 %all-to-all-done.4 = bf16[192,8,512]{2,0,1:T(8,128)(2,1)S(1)} async-done(((bf16[192,8,512]{2,0,1:T(8,128)(2,1)}), bf16[192,8,512]{2,0,1:T(8,128)(2,1)S(1)}, u32[]{:S(2)}, u32[]{:S(2)}) %all-to-all-start.4) | async-done | bytes 1572896 | tf_op jit(solution)/shard_map/all_to_all | solution.py:99
  402.2 0.9 stack.2
  403.2 3.5 all-to-all-start.5
  406.7 2.2 fusion.17
  409.0 1.8 fusion
  410.8 4.1 all_to_all.45
  414.9 4.9 all-to-all-done.5
  419.8 8.9 %all-to-all-start.3 = ((bf16[64,3,4096]{2,1,0:T(4,128)(2,1)}), bf16[64,3,4096]{2,1,0:T(4,128)(2,1)}, u32[]{:S(2)}, u32[]{:S(2)}) async-start(bf16[64,3,4096]{2,1,0:T(4,128)(2,1)} %all_to_all.45), calls=%async_computation.3 | async-start | bytes 4194304 | tf_op jit(solution)/shard_map/all_to_all | solution.py:96
  428.6 13.6 %all_gather.15 = bf16[1536,224]{1,0:T(8,128)(2,1)S(1)} all-gather(bf16[192,224]{1,0:T(8,128)(2,1)S(1)} %get-tuple-element.11), channel_id=1, replica_groups=mesh['dp'=8,'expert'=64] {'dp'}, dimensions={0}, use_global_device_ids=true | all-gather | bytes 774144 | tf_op jit(solution)/shard_map/all_gather | solution.py:112
  442.2 2.1 convolution_convert_fusion.1
  444.3 2.5 reduce_sum.49
  446.9 2.1 convolution_convert_fusion.2
  449.0 2.5 reduce_sum.48
  451.5 74.7 %all-to-all-done.3 = bf16[64,3,4096]{2,1,0:T(4,128)(2,1)} async-done(((bf16[64,3,4096]{2,1,0:T(4,128)(2,1)}), bf16[64,3,4096]{2,1,0:T(4,128)(2,1)}, u32[]{:S(2)}, u32[]{:S(2)}) %all-to-all-start.3) | async-done | bytes 1572896 | tf_op jit(solution)/shard_map/all_to_all | solution.py:96
  526.1 2.5 convert_reduce_fusion
  528.6 1.2 gather_fusion.5
  529.8 2.4 gather_fusion.4
  532.1 3.0 add_convert_fusion
  (43 shorter events, 3.2 us)
Async XLA Ops:
  7.2 6.2 %copy-start = (bf16[128,4096]{1,0:T(8,128)(2,1)S(1)}, bf16[128,4096]{1,0:T(8,128)(2,1)}, u32[]{:S(2)}) copy-start(bf16[128,4096]{1,0:T(8,128)(2,1)} %param.7) | copy-start | bytes 3145732
  7.2 127.9 %all-gather.6.cloned.1.call-start = ((), (), s32[]{:S(2)}) async-start(), calls=%async_computation.7 | async-start | bytes 2064384 | tf_op jit(solution)/shard_map/all_gather | solution.py:69
  16.4 116.1 %all-to-all-start = ((bf16[64,3,4096]{2,1,0:T(4,128)(2,1)}), bf16[64,3,4096]{2,1,0:T(4,128)(2,1)S(1)}, u32[]{:S(2)}, u32[]{:S(2)}) async-start(bf16[64,3,4096]{2,1,0:T(4,128)(2,1)} %broadcast_in_dim.87), calls=%async_computation | async-start | bytes 4194304 | tf_op jit(solution)/shard_map/all_to_all | solution.py:65
  35.2 102.6 %all-gather.4.cloned.1.call-start = ((), (), s32[]{:S(2)}) async-start(), calls=%async_computation.6 | async-start | bytes 2064384 | tf_op jit(solution)/shard_map/all_gather | solution.py:68
  35.9 105.2 %all-gather.8.cloned.1.call-start = ((), (), s32[]{:S(2)}) async-start(), calls=%async_computation.8 | async-start | bytes 2064384 | tf_op jit(solution)/shard_map/all_gather | solution.py:70
  148.6 8.6 %copy-start.4 = (f32[128,2]{0,1:T(2,128)S(1)}, f32[128,2]{0,1:T(2,128)}, u32[]{:S(2)}) copy-start(f32[128,2]{0,1:T(2,128)} %param.9) | copy-start | bytes 3076
  148.6 105.5 %all-to-all-start.1 = ((bf16[64,3,4096]{2,1,0:T(4,128)(2,1)}), bf16[64,3,4096]{2,1,0:T(4,128)(2,1)}, u32[]{:S(2)}, u32[]{:S(2)}) async-start(bf16[64,3,4096]{2,1,0:T(4,128)(2,1)} %all_to_all.41), calls=%async_computation.1 | async-start | bytes 4194304 | tf_op jit(solution)/shard_map/all_to_all | solution.py:80
  270.5 105.7 %all-to-all-start.2 = ((bf16[64,3,4096]{2,1,0:T(4,128)(2,1)}), bf16[64,3,4096]{2,1,0:T(4,128)(2,1)}, u32[]{:S(2)}, u32[]{:S(2)}) async-start(bf16[64,3,4096]{2,1,0:T(4,128)(2,1)} %broadcast_in_dim.92), calls=%async_computation.2 | async-start | bytes 4194304 | tf_op jit(solution)/shard_map/all_to_all | solution.py:88
  376.2 26.0 %all-to-all-start.4 = ((bf16[192,8,512]{2,0,1:T(8,128)(2,1)}), bf16[192,8,512]{2,0,1:T(8,128)(2,1)S(1)}, u32[]{:S(2)}, u32[]{:S(2)}) async-start(bf16[192,8,512]{2,0,1:T(8,128)(2,1)} %copy.20), calls=%async_computation.4 | async-start | bytes 3145728 | tf_op jit(solution)/shard_map/all_to_all | solution.py:99
  380.7 4.3 copy-start.2
  387.7 15.4 %copy-start.3 = (bf16[192,224]{1,0:T(8,128)(2,1)}, bf16[192,224]{1,0:T(8,128)(2,1)S(1)}, u32[]{:S(2)}) copy-start(bf16[192,224]{1,0:T(8,128)(2,1)S(1)} %get-tuple-element.12) | copy-start | bytes 258052
  403.2 16.6 %all-to-all-start.5 = ((bf16[8,192,224]{2,1,0:T(8,128)(2,1)}), bf16[8,192,224]{2,1,0:T(8,128)(2,1)S(1)}, u32[]{:S(2)}, u32[]{:S(2)}) async-start(bf16[8,192,224]{2,1,0:T(8,128)(2,1)} %stack.2), calls=%async_computation.5 | async-start | bytes 1572864 | tf_op jit(solution)/shard_map/all_to_all | solution.py:104
  406.7 2.3 copy-start.1
  419.8 106.4 %all-to-all-start.3 = ((bf16[64,3,4096]{2,1,0:T(4,128)(2,1)}), bf16[64,3,4096]{2,1,0:T(4,128)(2,1)}, u32[]{:S(2)}, u32[]{:S(2)}) async-start(bf16[64,3,4096]{2,1,0:T(4,128)(2,1)} %all_to_all.45), calls=%async_computation.3 | async-start | bytes 4194304 | tf_op jit(solution)/shard_map/all_to_all | solution.py:96
Sparse Core Ops, SparseCore 0:
  10.1 36.9 all-gather.5
  49.2 32.9 all-gather.3
  84.3 32.8 all-gather.7
